TPU v7x, 32 devices: a whole 2x2x4 slice. The times are simulated.
32 devices in a mesh: dp: 8 (over y, x, core), tensor: 4 (over z).
Axes of the slice: x: 2, y: 2, z: 4, core: 2. Of those that a mesh axis runs over, the one named last changes fastest.
Arguments:
- tokens: bfloat16 [8192, 2048], P(('dp', 'tensor')), may hold values from -6 to 6
- segments: int32 [8192], P('dp'), may hold values from 0 to 1023, as said below
- positions: int32 [8192], P('dp'), may hold values from 0 to 1023, as said below
- norm_attn: float32 [2048], replicated, may hold values from 0.25 to 1.75
- w_query: bfloat16 [2048, 2048], P('dp', 'tensor'), may hold values from -0.125 to 0.125
- w_key: bfloat16 [2048, 512], P('dp', 'tensor'), may hold values from -0.125 to 0.125
- w_value: bfloat16 [2048, 512], P('dp', 'tensor'), may hold values from -0.125 to 0.125
- w_out: bfloat16 [2048, 2048], P('tensor', 'dp'), may hold values from -0.375 to 0.375
- norm_mlp: float32 [2048], replicated, may hold values from 0.25 to 1.75
- w_gate: bfloat16 [2048, 8192], P('dp', 'tensor'), may hold values from -0.125 to 0.125
- w_up: bfloat16 [2048, 8192], P('dp', 'tensor'), may hold values from -0.125 to 0.125
- w_down: bfloat16 [8192, 2048], P('tensor', 'dp'), may hold values from -0.09375 to 0.09375
- cotangent: bfloat16 [8192, 2048], P(('dp', 'tensor')), may hold values from -6 to 6
Outputs:
- layer_out: bfloat16 [8192, 2048], P(('dp', 'tensor'))
- input_grad: float32 [8192, 2048], P(('dp', 'tensor'))
- grad_norm_attn: float32 [2048], replicated
- grad_query: float32 [2048, 2048], P('dp', 'tensor')
- grad_key: float32 [2048, 512], P('dp', 'tensor')
- grad_value: float32 [2048, 512], P('dp', 'tensor')
- grad_output: float32 [2048, 2048], P('tensor', 'dp')
- grad_norm_mlp: float32 [2048], replicated
- grad_gate: float32 [2048, 8192], P('dp', 'tensor')
- grad_up: float32 [2048, 8192], P('dp', 'tensor')
- grad_down: float32 [8192, 2048], P('tensor', 'dp')
Inputs may be any that keep to these rules, and one draw needn't show every extreme that they name: `segments`: within each sequence of 1024 tokens, a token's label is the place in that sequence of its document's first token, so labels never fall along a sequence; the first sequence of all is a single document, and the last token of the last sequence starts a document of its own. `positions`: each token's position counts from 0 at its document's first token.
All inputs are finite; a program needn't handle non-finite values.
Results may differ from a plain program's by a relative error of at most 0.022.
Values may be sent and summed in bfloat16 or wider, within the bound.
No kernel may reach another device: no remote copies, remote signals or barrier semaphores. Data moves between devices by JAX's collectives and lax.ppermute only.
A program may use at most 192 MiB of HBM per device.

v0:
```python
from functools import partial
import math
import jax
import jax.numpy as jnp
from jax import lax
from jax.sharding import PartitionSpec as P

QH = 32
KVH = 8
HD = 64
LEN = 1024


def rms_scale(values, norm_gain):
    inverse = lax.rsqrt(jnp.mean(values * values, axis=-1, keepdims=True) + 1e-05)
    return values * inverse * norm_gain


def rotary_tables(positions):
    freq_index = jnp.arange(HD // 2, dtype=jnp.int32).astype(jnp.float32)
    inverse = jnp.exp(freq_index * (-2.0 * math.log(500000.0) / HD))
    angles = positions.astype(jnp.float32)[:, None] * inverse[None, :]
    return (jnp.cos(angles), jnp.sin(angles))


def rotate(values, cosine_table, sine_table):
    half_width = values.shape[-1] // 2
    lower_half = values[..., :half_width]
    upper_half = values[..., half_width:]
    cosine_rows = cosine_table[:, None, :]
    sine_rows = sine_table[:, None, :]
    return jnp.concatenate(
        [
            lower_half * cosine_rows - upper_half * sine_rows,
            upper_half * cosine_rows + lower_half * sine_rows,
        ],
        axis=-1,
    )


def silu_product(gate_values, up_values):
    return jax.nn.silu(gate_values) * up_values


def local(
    tokens,
    segments,
    positions,
    norm_attn,
    w_query,
    w_key,
    w_value,
    w_out,
    norm_mlp,
    w_gate,
    w_up,
    w_down,
    cotangent,
):
    kv_local = w_key.shape[1] // HD
    per_group = QH // KVH
    block_rows = min(512, LEN)
    score_scale = 1.0 / math.sqrt(HD)
    inputs = tokens.astype(jnp.float32)
    normed_local = rms_scale(inputs, norm_attn).astype(jnp.bfloat16)
    normed_in = lax.all_gather(normed_local, "tensor", axis=0, tiled=True)
    query_all, key_all, value_all, out_all = (
        lax.all_gather(w_query, "dp", axis=0, tiled=True),
        lax.all_gather(w_key, "dp", axis=0, tiled=True),
        lax.all_gather(w_value, "dp", axis=0, tiled=True),
        lax.all_gather(w_out, "dp", axis=1, tiled=True),
    )
    group_rows = normed_in.shape[0]
    block_count = group_rows // block_rows
    cosine_table, sine_table = rotary_tables(positions)
    rotate_here = partial(rotate, cosine_table=cosine_table, sine_table=sine_table)
    query_raw = jnp.dot(normed_in, query_all, preferred_element_type=jnp.float32).reshape(
        group_rows, kv_local * per_group, HD
    )
    key_raw = jnp.dot(normed_in, key_all, preferred_element_type=jnp.float32).reshape(
        group_rows, kv_local, HD
    )
    all_queries = (
        rotate_here(query_raw).astype(jnp.bfloat16).reshape(group_rows, kv_local, per_group, HD)
    )
    all_keys = rotate_here(key_raw).astype(jnp.bfloat16)
    all_values = (
        jnp.dot(normed_in, value_all, preferred_element_type=jnp.float32)
        .astype(jnp.bfloat16)
        .reshape(group_rows, kv_local, HD)
    )
    place_index = jnp.arange(LEN, dtype=jnp.int32)

    def block_scores(block_index):
        row_start = block_index * block_rows
        seq_start = row_start // LEN * LEN
        query_rows = lax.dynamic_slice_in_dim(all_queries, row_start, block_rows, 0)
        query_segs = lax.dynamic_slice_in_dim(segments, row_start, block_rows, 0)
        query_place = row_start - seq_start + jnp.arange(block_rows, dtype=jnp.int32)
        allowed = (place_index[None, :] <= query_place[:, None]) & (
            segments[None, :] == query_segs[:, None]
        )
        scores = (
            jnp.einsum("qhgd,khd->hgqk", query_rows, all_keys, preferred_element_type=jnp.float32)
            * score_scale
        )
        return (jnp.where(allowed, scores, -1e30), query_rows, all_keys, all_values, seq_start)

    def forward_block(block_index):
        scores, query_rows, near_keys, near_values, seq_start = block_scores(block_index)
        row_peak = jnp.max(scores, axis=-1, keepdims=True)
        row_total = jnp.sum(jnp.exp(scores - row_peak), axis=-1, keepdims=True)
        log_total = row_peak + jnp.log(row_total)
        attn_probs = jnp.exp(scores - log_total).astype(jnp.bfloat16)
        context_block = jnp.einsum(
            "hgqk,khd->qhgd", attn_probs, near_values, preferred_element_type=jnp.float32
        )
        return (context_block.reshape(block_rows, -1).astype(jnp.bfloat16), log_total)

    context, log_totals = lax.map(forward_block, jnp.arange(block_count, dtype=jnp.int32))
    context = context.reshape(group_rows, -1)
    attn_branch = lax.psum_scatter(
        jnp.dot(context, out_all, preferred_element_type=jnp.float32).astype(jnp.bfloat16),
        "tensor",
        scatter_dimension=0,
        tiled=True,
    ).astype(jnp.float32)
    middle = inputs + attn_branch
    normed_mid_local = rms_scale(middle, norm_mlp).astype(jnp.bfloat16)
    normed_mid = lax.all_gather(normed_mid_local, "tensor", axis=0, tiled=True)
    gate_all, up_all, down_all = (
        lax.all_gather(w_gate, "dp", axis=0, tiled=True),
        lax.all_gather(w_up, "dp", axis=0, tiled=True),
        lax.all_gather(w_down, "dp", axis=1, tiled=True),
    )
    gate_values = jnp.dot(normed_mid, gate_all, preferred_element_type=jnp.float32)
    up_values = jnp.dot(normed_mid, up_all, preferred_element_type=jnp.float32)
    hidden = silu_product(gate_values, up_values).astype(jnp.bfloat16)
    mlp_branch = lax.psum_scatter(
        jnp.dot(hidden, down_all, preferred_element_type=jnp.float32).astype(jnp.bfloat16),
        "tensor",
        scatter_dimension=0,
        tiled=True,
    ).astype(jnp.float32)
    layer_out = (middle + mlp_branch).astype(jnp.bfloat16)
    cot_all = lax.all_gather(cotangent, "tensor", axis=0, tiled=True)
    d_hidden = jnp.einsum("rd,fd->rf", cot_all, down_all, preferred_element_type=jnp.float32)
    silu_back = jax.vjp(silu_product, gate_values, up_values)[1]
    d_gate32, d_up32 = silu_back(d_hidden)
    d_gate = d_gate32.astype(jnp.bfloat16)
    d_up = d_up32.astype(jnp.bfloat16)
    gate_part = jnp.einsum("rd,rf->df", normed_mid, d_gate, preferred_element_type=jnp.float32)
    up_part = jnp.einsum("rd,rf->df", normed_mid, d_up, preferred_element_type=jnp.float32)
    down_part = jnp.einsum("rf,rd->fd", hidden, cot_all, preferred_element_type=jnp.float32)
    d_normed_mid = lax.psum_scatter(
        (
            jnp.einsum("rf,df->rd", d_gate, gate_all, preferred_element_type=jnp.float32)
            + jnp.einsum("rf,df->rd", d_up, up_all, preferred_element_type=jnp.float32)
        ).astype(jnp.bfloat16),
        "tensor",
        scatter_dimension=0,
        tiled=True,
    ).astype(jnp.float32)
    mid_back = jax.vjp(rms_scale, middle, norm_mlp)[1]
    d_middle_norm, mlp_gain_part = mid_back(d_normed_mid)
    d_middle = cotangent.astype(jnp.float32) + d_middle_norm
    d_branch = lax.all_gather(d_middle.astype(jnp.bfloat16), "tensor", axis=0, tiled=True)
    out_part = jnp.einsum("rc,rd->cd", context, d_branch, preferred_element_type=jnp.float32)
    d_context = jnp.einsum(
        "rd,cd->rc", d_branch, out_all, preferred_element_type=jnp.float32
    ).astype(jnp.bfloat16)
    d_context = d_context.reshape(group_rows, kv_local, per_group, HD)

    def backward_block(grad_carry, block_index):
        key_grads, value_grads = grad_carry
        scores, query_rows, near_keys, near_values, seq_start = block_scores(block_index)
        probs_full = jnp.exp(scores - log_totals[block_index])
        attn_probs = probs_full.astype(jnp.bfloat16)
        d_rows = lax.dynamic_slice_in_dim(d_context, block_index * block_rows, block_rows, 0)
        d_probs = jnp.einsum(
            "qhgd,khd->hgqk", d_rows, near_values, preferred_element_type=jnp.float32
        )
        d_scores = (
            probs_full * (d_probs - jnp.sum(probs_full * d_probs, axis=-1, keepdims=True))
        ).astype(jnp.bfloat16)
        d_queries = (
            jnp.einsum("hgqk,khd->qhgd", d_scores, near_keys, preferred_element_type=jnp.float32)
            * score_scale
        )
        d_keys = (
            jnp.einsum("hgqk,qhgd->khd", d_scores, query_rows, preferred_element_type=jnp.float32)
            * score_scale
        )
        d_values = jnp.einsum(
            "hgqk,qhgd->khd", attn_probs, d_rows, preferred_element_type=jnp.float32
        )
        old_keys = key_grads
        key_grads = old_keys + d_keys
        old_values = value_grads
        value_grads = old_values + d_values
        return ((key_grads, value_grads), d_queries)

    empty_grads = jnp.zeros((group_rows, kv_local, HD), jnp.float32)
    kv_grads, query_grads = lax.scan(
        backward_block, (empty_grads, empty_grads), jnp.arange(block_count, dtype=jnp.int32)
    )
    query_grads = query_grads.reshape(group_rows, kv_local * per_group, HD)
    query_back = jax.vjp(rotate_here, query_raw)[1]
    key_back = jax.vjp(rotate_here, key_raw)[1]
    d_query_raw = query_back(query_grads)[0].astype(jnp.bfloat16).reshape(group_rows, -1)
    d_key_raw = key_back(kv_grads[0])[0].astype(jnp.bfloat16).reshape(group_rows, -1)
    d_value_raw = kv_grads[1].astype(jnp.bfloat16).reshape(group_rows, -1)
    query_part = jnp.einsum("rd,rc->dc", normed_in, d_query_raw, preferred_element_type=jnp.float32)
    key_part = jnp.einsum("rd,rc->dc", normed_in, d_key_raw, preferred_element_type=jnp.float32)
    value_part = jnp.einsum("rd,rc->dc", normed_in, d_value_raw, preferred_element_type=jnp.float32)
    query_rows = d_query_raw
    d_normed_in = lax.psum_scatter(
        (
            jnp.einsum("rc,dc->rd", query_rows, query_all, preferred_element_type=jnp.float32)
            + jnp.einsum("rc,dc->rd", d_key_raw, key_all, preferred_element_type=jnp.float32)
            + jnp.einsum("rc,dc->rd", d_value_raw, value_all, preferred_element_type=jnp.float32)
        ).astype(jnp.bfloat16),
        "tensor",
        scatter_dimension=0,
        tiled=True,
    ).astype(jnp.float32)
    in_back = jax.vjp(rms_scale, inputs, norm_attn)[1]
    d_input_norm, attn_gain_part = in_back(d_normed_in)
    input_grad = d_middle + d_input_norm
    grad_norm_attn, grad_norm_mlp = lax.psum((attn_gain_part, mlp_gain_part), ("dp", "tensor"))
    grad_query, grad_key, grad_value, grad_output, grad_gate, grad_up, grad_down = (
        lax.psum_scatter(
            query_part.astype(jnp.bfloat16), "dp", scatter_dimension=0, tiled=True
        ).astype(jnp.float32),
        lax.psum_scatter(
            key_part.astype(jnp.bfloat16), "dp", scatter_dimension=0, tiled=True
        ).astype(jnp.float32),
        lax.psum_scatter(
            value_part.astype(jnp.bfloat16), "dp", scatter_dimension=0, tiled=True
        ).astype(jnp.float32),
        lax.psum_scatter(
            out_part.astype(jnp.bfloat16), "dp", scatter_dimension=1, tiled=True
        ).astype(jnp.float32),
        lax.psum_scatter(
            gate_part.astype(jnp.bfloat16), "dp", scatter_dimension=0, tiled=True
        ).astype(jnp.float32),
        lax.psum_scatter(
            up_part.astype(jnp.bfloat16), "dp", scatter_dimension=0, tiled=True
        ).astype(jnp.float32),
        lax.psum_scatter(
            down_part.astype(jnp.bfloat16), "dp", scatter_dimension=1, tiled=True
        ).astype(jnp.float32),
    )
    return (
        layer_out,
        input_grad,
        grad_norm_attn,
        grad_query,
        grad_key,
        grad_value,
        grad_output,
        grad_norm_mlp,
        grad_gate,
        grad_up,
        grad_down,
    )


def solution(mesh):
    in_specs = (
        P(("dp", "tensor"), None),
        P("dp"),
        P("dp"),
        P(),
        P("dp", "tensor"),
        P("dp", "tensor"),
        P("dp", "tensor"),
        P("tensor", "dp"),
        P(),
        P("dp", "tensor"),
        P("dp", "tensor"),
        P("tensor", "dp"),
        P(("dp", "tensor"), None),
    )
    out_specs = (
        P(("dp", "tensor"), None),
        P(("dp", "tensor"), None),
        P(),
        P("dp", "tensor"),
        P("dp", "tensor"),
        P("dp", "tensor"),
        P("tensor", "dp"),
        P(),
        P("dp", "tensor"),
        P("dp", "tensor"),
        P("tensor", "dp"),
    )
    return jax.shard_map(local, mesh=mesh, in_specs=in_specs, out_specs=out_specs, check_vma=False)
```

profile of v0, /device:TPU:0, one launch (start us, length us, event | category | flops | bytes accessed | tf_op | source)
XLA Modules:
  0.0 1351.4 jit_solution(8502099795112230766)
XLA Ops:
  14.0 11.3 all_gather.35
  25.4 9.8 all_gather.36
  35.7 60.3 %all-gather.10.cloned.1.call-done = bf16[1024,2048]{1,0:T(8,128)(2,1)} async-done(((bf16[256,2048]{1,0:T(8,128)(2,1)}), bf16[1024,2048]{1,0:T(8,128)(2,1)}) %all-gather.10.cloned.1.call-update) | async-done | bytes 4194320 | tf_op jit(solution)/shard_map/all_gather | solution.py:66
  99.8 24.4 %all-gather.12.cloned.1.call-done = bf16[2048,512]{1,0:T(8,128)(2,1)} async-done(((bf16[256,512]{1,0:T(8,128)(2,1)}), bf16[2048,512]{1,0:T(8,128)(2,1)}) %all-gather.12.cloned.1.call-update) | async-done | bytes 2097168 | tf_op jit(solution)/shard_map/all_gather | solution.py:68
  124.2 5.2 fusion.75
  133.2 30.5 %while.32 = (s32[]{:T(128)}, bf16[2,512,512]{2,1,0:T(8,128)(2,1)}, f32[2,2,4,512,1]{3,2,1,4,0:T(4,128)}, s32[2]{0:T(128)S(1)}, s32[1024]{0:T(1024)S(1)}, /*index...) while((s32[]{:T(128)}, bf16[2,512,512]{2,1,0:T(8,128)(2,1)}, ...), condition=%wide.region_4.5_spmd.clone, body=%wide.region_1.4_spmd.clone.sunk | while | flops 1121710592 | bytes 56244616 | solution.py:120
  143.2 4.4 fusion.150
  163.7 6.9 convolution_convert_fusion.4
  171.3 76.3 %reduce-scatter.12.cloned.1.call-done = bf16[256,2048]{1,0:T(8,128)(2,1)} async-done(((bf16[1024,2048]{1,0:T(8,128)(2,1)}), bf16[256,2048]{1,0:T(8,128)(2,1)}) %reduce-scatter.12.cloned.1.call-update) | async-done | bytes 1048592 | tf_op jit(solution)/shard_map/reduce_scatter | solution.py:122
  254.2 50.0 %all-gather.20.cloned.1.call-done = bf16[2048,2048]{1,0:T(8,128)(2,1)} async-done(((bf16[256,2048]{1,0:T(8,128)(2,1)}), bf16[2048,2048]{1,0:T(8,128)(2,1)}) %all-gather.20.cloned.1.call-update) | async-done | bytes 8388624 | tf_op jit(solution)/shard_map/all_gather | solution.py:133
  304.1 82.8 %all-gather.16.cloned.1.call-done = bf16[1024,2048]{1,0:T(8,128)(2,1)} async-done(((bf16[256,2048]{1,0:T(8,128)(2,1)}), bf16[1024,2048]{1,0:T(8,128)(2,1)}) %all-gather.16.cloned.1.call-update) | async-done | bytes 4194320 | tf_op jit(solution)/shard_map/all_gather | solution.py:130
  386.9 14.9 %fusion.78 = f32[1024,2048]{1,0:T(8,128)} fusion(bf16[1024,2048]{1,0:T(8,128)(2,1)} %all-gather.16.cloned.1.call-done, bf16[2048,2048]{1,0:T(8,128)(2,1)} %all-gather.20.cloned.1.call-done), kind=kOutput, calls=%fused_computation.135 | convolution fusion | flops 8589934592 | bytes 20971520 | tf_op jit(solution)/shard_map/dot_general | solution.py:137
  401.8 39.8 %all-gather.18.cloned.1.call-done = bf16[2048,2048]{1,0:T(8,128)(2,1)} async-done(((bf16[256,2048]{1,0:T(8,128)(2,1)}), bf16[2048,2048]{1,0:T(8,128)(2,1)}) %all-gather.18.cloned.1.call-update) | async-done | bytes 8388624 | tf_op jit(solution)/shard_map/all_gather | solution.py:132
  441.6 14.4 %fusion.77 = f32[1024,2048]{1,0:T(8,128)} fusion(bf16[1024,2048]{1,0:T(8,128)(2,1)} %all-gather.16.cloned.1.call-done, bf16[2048,2048]{1,0:T(8,128)(2,1)} %all-gather.18.cloned.1.call-done), kind=kOutput, calls=%fused_computation.134 | convolution fusion | flops 8589934592 | bytes 20971520 | tf_op jit(solution)/shard_map/dot_general | solution.py:136
  455.9 67.9 %all-gather.24.cloned.1.call-done = bf16[1024,2048]{1,0:T(8,128)(2,1)} async-done(((bf16[256,2048]{1,0:T(8,128)(2,1)}), bf16[1024,2048]{1,0:T(8,128)(2,1)}) %all-gather.24.cloned.1.call-update) | async-done | bytes 4194320 | tf_op jit(solution)/shard_map/all_gather | solution.py:146
  523.9 56.3 %all-gather.22.cloned.1.call-done = bf16[2048,2048]{1,0:T(8,128)(2,1)} async-done(((bf16[2048,256]{1,0:T(8,128)(2,1)}), bf16[2048,2048]{1,0:T(8,128)(2,1)}) %all-gather.22.cloned.1.call-update) | async-done | bytes 8388624 | tf_op jit(solution)/shard_map/all_gather | solution.py:134
  580.2 21.8 %multiply_convert_fusion = (bf16[1024,2048]{1,0:T(8,128)(2,1)}, bf16[1024,2048]{1,0:T(8,128)(2,1)}, bf16[1024,2048]{1,0:T(8,128)(2,1)}) fusion(f32[1024,2048]{1,0:T(8,128)} %fusion.77, f32[1024,2048]{1,0:T(8,128)} %fusion.78, bf16[1024,2048]{1,0:T(8,128)(2,1)} %all-gather.24.cloned.1.call-done, bf16[2048,2048]{1,0:T(8,128)(2,1)} %all-gather.22.cloned.1.call-done), kind=kOutput, calls=%fused_computation.69 | convolution fusion | flops 8623489024 | bytes 41943040 | tf_op jit(solution)/shard_map/rd,fd->rf/dot_general | solution.py:147
  602.0 12.9 fusion.79
  614.9 12.9 add_convert_fusion.1
  627.9 76.9 %reduce-scatter.16.cloned.1.call-done = bf16[256,2048]{1,0:T(8,128)(2,1)} async-done(((bf16[1024,2048]{1,0:T(8,128)(2,1)}), bf16[256,2048]{1,0:T(8,128)(2,1)}) %reduce-scatter.16.cloned.1.call-update) | async-done | bytes 1048592 | tf_op jit(solution)/shard_map/reduce_scatter | solution.py:155
  710.8 14.4 %convolution_convert_fusion.1 = bf16[2048,2048]{1,0:T(8,128)(2,1)} fusion(bf16[1024,2048]{1,0:T(8,128)(2,1)} %all-gather.16.cloned.1.call-done, bf16[1024,2048]{1,0:T(8,128)(2,1)} %get-tuple-element.389), kind=kOutput, calls=%fused_computation.74 | convolution fusion | flops 8594128896 | bytes 16777216 | tf_op jit(solution)/shard_map/rd,rf->df/dot_general | solution.py:153
  725.3 14.1 %convolution_convert_fusion.2 = bf16[2048,2048]{1,0:T(8,128)(2,1)} fusion(bf16[1024,2048]{1,0:T(8,128)(2,1)} %all-gather.16.cloned.1.call-done, bf16[1024,2048]{1,0:T(8,128)(2,1)} %get-tuple-element.390), kind=kOutput, calls=%fused_computation.75 | convolution fusion | flops 8594128896 | bytes 16777216 | tf_op jit(solution)/shard_map/rd,rf->df/dot_general | solution.py:152
  739.5 14.1 %convolution_convert_fusion = bf16[2048,2048]{1,0:T(8,128)(2,1)} fusion(bf16[1024,2048]{1,0:T(8,128)(2,1)} %get-tuple-element.391, bf16[1024,2048]{1,0:T(8,128)(2,1)} %all-gather.24.cloned.1.call-done), kind=kOutput, calls=%fused_computation.73 | convolution fusion | flops 8594128896 | bytes 16777216 | tf_op jit(solution)/shard_map/rf,rd->fd/dot_general | solution.py:154
  753.7 38.5 %all-gather.26.cloned.1.call-done = bf16[1024,2048]{1,0:T(8,128)(2,1)} async-done(((bf16[256,2048]{1,0:T(8,128)(2,1)}), bf16[1024,2048]{1,0:T(8,128)(2,1)}) %all-gather.26.cloned.1.call-update) | async-done | bytes 4194320 | tf_op jit(solution)/shard_map/all_gather | solution.py:167
  792.2 5.5 convolution_convert_fusion.9
  797.7 133.2 %while.33 = (s32[]{:T(128)}, f32[1024,2,64]{0,2,1:T(8,128)}, f32[1024,2,64]{0,2,1:T(8,128)}, f32[2,512,2,4,64]{1,0,4,3,2:T(2,128)}, s32[2]{0:T(128)S(1)}, /*inde...) while((s32[]{:T(128)}, f32[1024,2,64]{0,2,1:T(8,128)}, ...), condition=%wide.region_12.13_spmd.clone, body=%wide.region_10.12_spmd.clone.sunk | while | flops 2749755904 | bytes 184482448 | solution.py:204
  806.1 5.3 fusion.164
  811.4 11.0 fusion.161
  822.3 8.5 fusion.162
  836.6 6.1 fusion.165
  843.8 19.7 %dynamic_update_slice.31 = f32[2,512,2,4,64]{1,0,4,3,2:T(2,128)} dynamic-update-slice(f32[2,512,2,4,64]{1,0,4,3,2:T(2,128)} %get-tuple-element.599, f32[1,512,2,4,64]{1,0,4,3,2:T(1,128)S(1)} %copy.49, s32[]{:T(128)S(6)} %copy.66, s32[]{:T(128)} %constant.161.clone.1..sunk.1, s32[]{:T(128)} %constant.161.clone.1..sunk.1, s32[]{:T(128)} %constant.161.clone.1..sunk.1, s32[]{:T(128)} %constant.161.clone.1..sunk.1) | dynamic-update-slice | bytes 2097156 | tf_op jit(solution)/shard_map/while/body/jit(dynamic_update_index_in_dim)/dynamic_update_slice | solution.py:204
  871.5 6.3 fusion.164
  877.8 11.1 fusion.161
  889.0 9.0 fusion.162
  903.7 6.2 fusion.165
  911.0 19.7 %dynamic_update_slice.31 = f32[2,512,2,4,64]{1,0,4,3,2:T(2,128)} dynamic-update-slice(f32[2,512,2,4,64]{1,0,4,3,2:T(2,128)} %get-tuple-element.599, f32[1,512,2,4,64]{1,0,4,3,2:T(1,128)S(1)} %copy.49, s32[]{:T(128)S(6)} %copy.66, s32[]{:T(128)} %constant.161.clone.1..sunk.1, s32[]{:T(128)} %constant.161.clone.1..sunk.1, s32[]{:T(128)} %constant.161.clone.1..sunk.1, s32[]{:T(128)} %constant.161.clone.1..sunk.1) | dynamic-update-slice | bytes 2097156 | tf_op jit(solution)/shard_map/while/body/jit(dynamic_update_index_in_dim)/dynamic_update_slice | solution.py:204
  936.6 4.5 convolution_convert_fusion.8
  941.2 5.9 convolution_convert_fusion.5
  965.3 13.9 %convolution_convert_fusion.3 = bf16[1024,2048]{1,0:T(8,128)(2,1)} fusion(bf16[1024,2048]{1,0:T(8,128)(2,1)} %get-tuple-element.391, bf16[2048,2048]{1,0:T(8,128)(2,1)} %all-gather.22.cloned.1.call-done), kind=kOutput, calls=%fused_computation.81 | convolution fusion | flops 8592031744 | bytes 16777216 | tf_op jit(solution)/shard_map/dot_general | solution.py:140
  984.9 30.2 %reduce-scatter.32.cloned.1.call-done = bf16[2048,256]{1,0:T(8,128)(2,1)} async-done(((bf16[2048,2048]{1,0:T(8,128)(2,1)}), bf16[2048,256]{1,0:T(8,128)(2,1)}) %reduce-scatter.32.cloned.1.call-update) | async-done | bytes 1048592 | tf_op jit(solution)/shard_map/reduce_scatter | solution.py:250
  1017.9 35.0 %reduce-scatter.24.cloned.1.call-done = bf16[256,128]{1,0:T(8,128)(2,1)} async-done(((bf16[2048,128]{1,0:T(8,128)(2,1)}), bf16[256,128]{1,0:T(8,128)(2,1)}) %reduce-scatter.24.cloned.1.call-update) | async-done | bytes 65552 | tf_op jit(solution)/shard_map/reduce_scatter | solution.py:238
  1054.3 36.1 %reduce-scatter.22.cloned.1.call-done = bf16[256,128]{1,0:T(8,128)(2,1)} async-done(((bf16[2048,128]{1,0:T(8,128)(2,1)}), bf16[256,128]{1,0:T(8,128)(2,1)}) %reduce-scatter.22.cloned.1.call-update) | async-done | bytes 65552 | tf_op jit(solution)/shard_map/reduce_scatter | solution.py:235
  1092.0 42.8 %reduce-scatter.26.cloned.1.call-done = bf16[512,256]{1,0:T(8,128)(2,1)} async-done(((bf16[512,2048]{1,0:T(8,128)(2,1)}), bf16[512,256]{1,0:T(8,128)(2,1)}) %reduce-scatter.26.cloned.1.call-update) | async-done | bytes 262160 | tf_op jit(solution)/shard_map/reduce_scatter | solution.py:241
  1136.5 43.1 %reduce-scatter.20.cloned.1.call-done = bf16[256,512]{1,0:T(8,128)(2,1)} async-done(((bf16[2048,512]{1,0:T(8,128)(2,1)}), bf16[256,512]{1,0:T(8,128)(2,1)}) %reduce-scatter.20.cloned.1.call-update) | async-done | bytes 262160 | tf_op jit(solution)/shard_map/reduce_scatter | solution.py:232
  1181.4 77.3 %reduce-scatter.18.cloned.1.call-done = bf16[256,2048]{1,0:T(8,128)(2,1)} async-done(((bf16[1024,2048]{1,0:T(8,128)(2,1)}), bf16[256,2048]{1,0:T(8,128)(2,1)}) %reduce-scatter.18.cloned.1.call-update) | async-done | bytes 1048592 | tf_op jit(solution)/shard_map/reduce_scatter | solution.py:217
  1261.0 45.8 %all-reduce.4 = (f32[2048]{0:T(1024)}, f32[2048]{0:T(1024)}) all-reduce(f32[2048]{0:T(1024)S(1)} %get-tuple-element.341, f32[2048]{0:T(1024)S(1)} %copy-done.35), channel_id=1, replica_groups=mesh['dp'=8,'tensor'=4] {'dp','tensor'}, use_global_device_ids=true, to_apply=%region_16.17 | all-reduce | flops 4096 | bytes 32768 | tf_op jit(solution)/shard_map/psum | solution.py:230
  1306.8 32.4 %reduce-scatter.14.cloned.1.call-done = bf16[256,2048]{1,0:T(8,128)(2,1)} async-done(((bf16[1024,2048]{1,0:T(8,128)(2,1)}), bf16[256,2048]{1,0:T(8,128)(2,1)}) %reduce-scatter.14.cloned.1.call-update) | async-done | bytes 1048592 | tf_op jit(solution)/shard_map/reduce_scatter | solution.py:139
  1339.3 5.1 fusion.69
  (233 shorter events, 118.1 us)
Async XLA Ops:
  7.2 18.2 %copy-start.34 = (bf16[256,128]{1,0:T(8,128)(2,1)S(1)}, bf16[256,128]{1,0:T(8,128)(2,1)}, u32[]{:S(2)}) copy-start(bf16[256,128]{1,0:T(8,128)(2,1)} %param.23) | copy-start | bytes 196612
  7.2 88.8 %all-gather.10.cloned.1.call-start = ((), (), s32[]{:S(2)}) async-start(), calls=%async_computation.11 | async-start | bytes 5242880 | tf_op jit(solution)/shard_map/all_gather | solution.py:66
  12.4 111.8 %all-gather.12.cloned.1.call-start = ((), (), s32[]{:S(2)}) async-start(), calls=%async_computation.12 | async-start | bytes 2359296 | tf_op jit(solution)/shard_map/all_gather | solution.py:68
  13.2 150.5 %all-gather.14.cloned.1.call-start = ((), (), s32[]{:S(2)}) async-start(), calls=%async_computation.13 | async-start | bytes 2359296 | tf_op jit(solution)/shard_map/all_gather | solution.py:71
  13.9 233.7 %reduce-scatter.12.cloned.1.call-start = ((), (), s32[]{:S(2)}) async-start(), calls=%async_computation.14 | async-start | bytes 5242880 | tf_op jit(solution)/shard_map/reduce_scatter | solution.py:122
  25.4 104.1 %copy-start.21 = (bf16[2048,128]{1,0:T(8,128)(2,1)}, bf16[2048,128]{1,0:T(8,128)(2,1)S(1)}, u32[]{:S(2)}) copy-start(bf16[2048,128]{1,0:T(8,128)(2,1)S(1)} %all_gather.35) | copy-start | bytes 1572868
  35.2 94.8 %copy-start.19 = (bf16[2048,128]{1,0:T(8,128)(2,1)}, bf16[2048,128]{1,0:T(8,128)(2,1)S(1)}, u32[]{:S(2)}) copy-start(bf16[2048,128]{1,0:T(8,128)(2,1)S(1)} %all_gather.36) | copy-start | bytes 1572868
  35.7 93.8 %copy-start.24 = (f32[1024,32]{0,1:T(8,128)}, f32[1024,32]{0,1:T(8,128)S(1)}, u32[]{:S(2)}) copy-start(f32[1024,32]{0,1:T(8,128)S(1)} %get-tuple-element.402) | copy-start | bytes 393220
  35.7 93.8 %copy-start.26 = (f32[1024,32]{0,1:T(8,128)}, f32[1024,32]{0,1:T(8,128)S(1)}, u32[]{:S(2)}) copy-start(f32[1024,32]{0,1:T(8,128)S(1)} %get-tuple-element.403) | copy-start | bytes 393220
  170.6 77.0 %copy-start.5 = (bf16[256,2048]{1,0:T(8,128)(2,1)S(1)}, bf16[256,2048]{1,0:T(8,128)(2,1)}, u32[]{:S(2)}) copy-start(bf16[256,2048]{1,0:T(8,128)(2,1)} %param.17) | copy-start | bytes 3145732
  170.6 78.6 %copy-start.30 = (f32[2048]{0:T(1024)S(1)}, f32[2048]{0:T(1024)}, u32[]{:S(2)}) copy-start(f32[2048]{0:T(1024)} %param.25) | copy-start | bytes 24580
  170.7 133.5 %all-gather.20.cloned.1.call-start = ((), (), s32[]{:S(2)}) async-start(), calls=%async_computation.17 | async-start | bytes 9437184 | tf_op jit(solution)/shard_map/all_gather | solution.py:133
  171.2 215.6 %all-gather.16.cloned.1.call-start = ((), (), s32[]{:S(2)}) async-start(), calls=%async_computation.15 | async-start | bytes 5242880 | tf_op jit(solution)/shard_map/all_gather | solution.py:130
  249.2 458.3 %copy-start.36 = (f32[256]{0:T(256)}, f32[256]{0:T(256)S(1)}, u32[]{:S(2)}) copy-start(f32[256]{0:T(256)S(1)} %fusion.73) | copy-start | bytes 3076
  251.9 189.7 %all-gather.18.cloned.1.call-start = ((), (), s32[]{:S(2)}) async-start(), calls=%async_computation.16 | async-start | bytes 9437184 | tf_op jit(solution)/shard_map/all_gather | solution.py:132
  252.6 271.3 %all-gather.24.cloned.1.call-start = ((), (), s32[]{:S(2)}) async-start(), calls=%async_computation.20 | async-start | bytes 5242880 | tf_op jit(solution)/shard_map/all_gather | solution.py:146
  253.4 326.8 %all-gather.22.cloned.1.call-start = ((), (), s32[]{:S(2)}) async-start(), calls=%async_computation.18 | async-start | bytes 9437184 | tf_op jit(solution)/shard_map/all_gather | solution.py:134
  254.1 450.7 %reduce-scatter.16.cloned.1.call-start = ((), (), s32[]{:S(2)}) async-start(), calls=%async_computation.21 | async-start | bytes 5242880 | tf_op jit(solution)/shard_map/reduce_scatter | solution.py:155
  602.0 12.9 copy-start.48
  627.8 77.0 %copy-start.10 = (bf16[256,2048]{1,0:T(8,128)(2,1)S(1)}, bf16[256,2048]{1,0:T(8,128)(2,1)}, u32[]{:S(2)}) copy-start(bf16[256,2048]{1,0:T(8,128)(2,1)} %reduce-scatter.12.cloned.1.call-done) | copy-start | bytes 3145732
  627.8 79.8 %copy-start.16 = (bf16[256,2048]{1,0:T(8,128)(2,1)S(1)}, bf16[256,2048]{1,0:T(8,128)(2,1)}, u32[]{:S(2)}) copy-start(bf16[256,2048]{1,0:T(8,128)(2,1)} %param.29) | copy-start | bytes 3145732
  627.8 164.4 %all-gather.26.cloned.1.call-start = ((), (), s32[]{:S(2)}) async-start(), calls=%async_computation.22 | async-start | bytes 5242880 | tf_op jit(solution)/shard_map/all_gather | solution.py:167
  707.6 17.7 %copy-start.40 = (f32[256]{0:T(256)}, f32[256]{0:T(256)S(1)}, u32[]{:S(2)}) copy-start(f32[256]{0:T(256)S(1)} %multiply_multiply_fusion.1) | copy-start | bytes 3076
  710.8 268.4 %reduce-scatter.30.cloned.1.call-start = ((), (), s32[]{:S(2)}) async-start(), calls=%async_computation.29 | async-start | bytes 9437184 | tf_op jit(solution)/shard_map/reduce_scatter | solution.py:247
  725.3 256.7 %reduce-scatter.28.cloned.1.call-start = ((), (), s32[]{:S(2)}) async-start(), calls=%async_computation.28 | async-start | bytes 9437184 | tf_op jit(solution)/shard_map/reduce_scatter | solution.py:244
  739.5 275.7 %reduce-scatter.32.cloned.1.call-start = ((), (), s32[]{:S(2)}) async-start(), calls=%async_computation.30 | async-start | bytes 9437184 | tf_op jit(solution)/shard_map/reduce_scatter | solution.py:250
  753.6 38.6 %copy-start.46 = (bf16[512,2048]{1,0:T(8,128)(2,1)S(1)}, bf16[512,2048]{1,0:T(8,128)(2,1)}, u32[]{:S(2)}) copy-start(bf16[512,2048]{1,0:T(8,128)(2,1)} %all-gather.14.cloned.1.call-done) | copy-start | bytes 6291460
  753.6 44.1 %copy-start.4 = (bf16[1024,2,64]{0,2,1:T(8,128)(2,1)S(1)}, bf16[1024,2,64]{0,2,1:T(8,128)(2,1)}, u32[]{:S(2)}) copy-start(bf16[1024,2,64]{0,2,1:T(8,128)(2,1)} %copy-done.3) | copy-start | bytes 786436
  753.6 44.1 %copy-start.15 = (bf16[1024,2,64]{0,2,1:T(8,128)(2,1)S(1)}, bf16[1024,2,64]{0,2,1:T(8,128)(2,1)}, u32[]{:S(2)}) copy-start(bf16[1024,2,64]{0,2,1:T(8,128)(2,1)} %copy-done.14) | copy-start | bytes 786436
  753.7 44.0 %copy-start.29 = (s32[1024]{0:T(1024)S(1)}, s32[1024]{0:T(1024)}, u32[]{:S(2)}) copy-start(s32[1024]{0:T(1024)} %param.18) | copy-start | bytes 12292
  753.7 299.1 %reduce-scatter.24.cloned.1.call-start = ((), (), s32[]{:S(2)}) async-start(), calls=%async_computation.26 | async-start | bytes 589824 | tf_op jit(solution)/shard_map/reduce_scatter | solution.py:238
  889.0 12.3 copy-start.2
  889.0 12.3 copy-start.7
  936.4 154.0 %reduce-scatter.22.cloned.1.call-start = ((), (), s32[]{:S(2)}) async-start(), calls=%async_computation.25 | async-start | bytes 589824 | tf_op jit(solution)/shard_map/reduce_scatter | solution.py:235
  941.2 193.6 %reduce-scatter.26.cloned.1.call-start = ((), (), s32[]{:S(2)}) async-start(), calls=%async_computation.27 | async-start | bytes 2359296 | tf_op jit(solution)/shard_map/reduce_scatter | solution.py:241
  947.1 232.5 %reduce-scatter.20.cloned.1.call-start = ((), (), s32[]{:S(2)}) async-start(), calls=%async_computation.24 | async-start | bytes 2359296 | tf_op jit(solution)/shard_map/reduce_scatter | solution.py:232
  956.9 301.8 %reduce-scatter.18.cloned.1.call-start = ((), (), s32[]{:S(2)}) async-start(), calls=%async_computation.23 | async-start | bytes 5242880 | tf_op jit(solution)/shard_map/reduce_scatter | solution.py:217
  965.2 374.0 %reduce-scatter.14.cloned.1.call-start = ((), (), s32[]{:S(2)}) async-start(), calls=%async_computation.19 | async-start | bytes 5242880 | tf_op jit(solution)/shard_map/reduce_scatter | solution.py:139
  982.0 276.7 %copy-start.6 = (bf16[256,2048]{1,0:T(8,128)(2,1)S(1)}, bf16[256,2048]{1,0:T(8,128)(2,1)}, u32[]{:S(2)}) copy-start(bf16[256,2048]{1,0:T(8,128)(2,1)} %param.17) | copy-start | bytes 3145732
  982.0 276.7 %copy-start.32 = (f32[2048]{0:T(1024)S(1)}, f32[2048]{0:T(1024)}, u32[]{:S(2)}) copy-start(f32[2048]{0:T(1024)} %param.20) | copy-start | bytes 24580
  982.0 276.7 %copy-start.39 = (f32[256]{0:T(256)S(1)}, f32[256]{0:T(256)}, u32[]{:S(2)}) copy-start(f32[256]{0:T(256)} %copy-done.38) | copy-start | bytes 3076
  984.9 276.1 %copy-start.35 = (f32[2048]{0:T(1024)S(1)}, f32[2048]{0:T(1024)}, u32[]{:S(2)}) copy-start(f32[2048]{0:T(1024)} %get-tuple-element.339) | copy-start | bytes 24580
  984.9 321.9 %copy-start.43 = (f32[256]{0:T(256)S(1)}, f32[256]{0:T(256)}, u32[]{:S(2)}) copy-start(f32[256]{0:T(256)} %copy-done.42) | copy-start | bytes 3076
  984.9 354.3 %copy-start.11 = (bf16[256,2048]{1,0:T(8,128)(2,1)S(1)}, bf16[256,2048]{1,0:T(8,128)(2,1)}, u32[]{:S(2)}) copy-start(bf16[256,2048]{1,0:T(8,128)(2,1)} %reduce-scatter.12.cloned.1.call-done) | copy-start | bytes 3145732
  984.9 354.3 %copy-start.17 = (bf16[256,2048]{1,0:T(8,128)(2,1)S(1)}, bf16[256,2048]{1,0:T(8,128)(2,1)}, u32[]{:S(2)}) copy-start(bf16[256,2048]{1,0:T(8,128)(2,1)} %param.29) | copy-start | bytes 3145732
  984.9 354.3 %copy-start.31 = (f32[2048]{0:T(1024)S(1)}, f32[2048]{0:T(1024)}, u32[]{:S(2)}) copy-start(f32[2048]{0:T(1024)} %param.25) | copy-start | bytes 24580
  984.9 354.3 %copy-start.37 = (f32[256]{0:T(256)S(1)}, f32[256]{0:T(256)}, u32[]{:S(2)}) copy-start(f32[256]{0:T(256)} %copy-done.36) | copy-start | bytes 3076
  984.9 354.3 %copy-start.41 = (f32[256]{0:T(256)S(1)}, f32[256]{0:T(256)}, u32[]{:S(2)}) copy-start(f32[256]{0:T(256)} %copy-done.40) | copy-start | bytes 3076
  (27 other events, 121.2 us)
Sparse Core Ops, SparseCore 0:
  12.6 83.4 all-gather.9
  97.9 26.2 all-gather.11
  126.1 28.1 all-gather.13
  170.8 76.7 reduce-scatter.11
  249.3 54.7 all-gather.19
  306.1 80.7 all-gather.15
  388.8 52.7 all-gather.17
  443.1 80.7 all-gather.23
  525.8 54.3 all-gather.21
  627.9 76.7 reduce-scatter.15
  710.9 81.2 all-gather.25
  795.5 69.9 reduce-scatter.29
  869.0 71.4 reduce-scatter.27
  943.8 71.2 reduce-scatter.31
  1018.7 34.1 reduce-scatter.23
  1056.3 34.0 reduce-scatter.21
  1093.6 41.1 reduce-scatter.25
  1138.5 41.0 reduce-scatter.19
  1181.9 76.7 reduce-scatter.17
  1260.9 78.3 reduce-scatter.13
where the time goes:
time: 1360 us; the launch traced here: 1350 us
  waiting for transfers between devices  874 us (64%)
  matrix products  253 us (19%)
  other arithmetic  68.7 us (5%)
  blocking collectives  67 us (5%)
  local copies, waits for them, and re-layouts  65 us (5%)
  between operations  15.1 us (1%)
    all_gather x1, waiting for transfers between devices, local(): normed_mid = lax.all_gather(normed_mid_local, 'tensor', axis=0, tiled=True)  82.8 us
    reduce_scatter x1, waiting for transfers between devices, local(): lax.psum_scatter((jnp.einsum('rc,dc->rd', query_rows, query_all, preferre...  77.3 us
    reduce_scatter x1, waiting for transfers between devices, local(): lax.psum_scatter((jnp.einsum('rf,df->rd', d_gate, gate_all, preferred_ele...  76.9 us
    reduce_scatter x1, waiting for transfers between devices, local(): lax.psum_scatter(jnp.dot(context, out_all, preferred_element_type=jnp.flo...  76.3 us
    all_gather x1, waiting for transfers between devices, local(): cot_all = lax.all_gather(cotangent, 'tensor', axis=0, tiled=True)  67.9 us
    all_gather x1, waiting for transfers between devices, local(): normed_in = lax.all_gather(normed_local, 'tensor', axis=0, tiled=True)  60.3 us
    all_gather x1, waiting for transfers between devices, local(): lax.all_gather(w_down, 'dp', axis=1, tiled=True)  56.3 us
    all_gather x1, waiting for transfers between devices, local(): lax.all_gather(w_up, 'dp', axis=0, tiled=True)  50 us
  transfers between devices with their start and end apart: 20, of which 17 were waited for; matrix products, arithmetic and copies ran while one was open for 22% of the time, Pallas kernels for 0%

commit v1 on v0

--- a/solution.py
+++ b/solution.py
@@ -9,6 +9,19 @@
 KVH = 8
 HD = 64
 LEN = 1024
+
+
+def ring_gather(x, axis, dim):
+    ways = lax.axis_size(axis)
+    up = [(d, (d + 1) % ways) for d in range(ways)]
+    down = [(d, (d - 1) % ways) for d in range(ways)]
+    earlier, later = ([x], [x])
+    for _ in range(ways // 2):
+        earlier.append(lax.ppermute(earlier[-1], axis, up))
+    for _ in range((ways - 1) // 2):
+        later.append(lax.ppermute(later[-1], axis, down))
+    line = jnp.concatenate([*earlier[::-1], *later[1:]], axis=dim)
+    return jnp.roll(line, (lax.axis_index(axis) - ways // 2) * x.shape[dim], axis=dim)
 
 
 def rms_scale(values, norm_gain):
@@ -164,7 +177,7 @@
     mid_back = jax.vjp(rms_scale, middle, norm_mlp)[1]
     d_middle_norm, mlp_gain_part = mid_back(d_normed_mid)
     d_middle = cotangent.astype(jnp.float32) + d_middle_norm
-    d_branch = lax.all_gather(d_middle.astype(jnp.bfloat16), "tensor", axis=0, tiled=True)
+    d_branch = ring_gather(d_middle.astype(jnp.bfloat16), "tensor", 0)
     out_part = jnp.einsum("rc,rd->cd", context, d_branch, preferred_element_type=jnp.float32)
     d_context = jnp.einsum(
         "rd,cd->rc", d_branch, out_all, preferred_element_type=jnp.float32

time: 1360 us -> 1500 us (1.10)
  waiting for transfers between devices: 874 us -> 1000 us
    reduce_scatter x1, waiting for transfers between devices: 0.01 us -> 72 us  [local(): lax.psum_scatter(gate_part.astype(jnp.bfloat16), 'dp', scatter_dimension=...]
    ppermute x0 -> x3, waiting for transfers between devices: none -> 66.4 us  [the longest x2 49.1 us: ring_gather(): earlier.append(lax.ppermute(earlier[-1], axis, up))]
    reduce_scatter x1, waiting for transfers between devices: 0.02 us -> 58 us  [local(): lax.psum_scatter(up_part.astype(jnp.bfloat16), 'dp', scatter_dimension=0,...]
    reduce_scatter x1, waiting for transfers between devices: 30.2 us -> 71.8 us  [local(): lax.psum_scatter(down_part.astype(jnp.bfloat16), 'dp', scatter_dimension=...]
    all_gather x1 -> x0, waiting for transfers between devices: 38.5 us -> none  [local(): lax.all_gather(d_middle.astype(jnp.bfloat16), 'tensor', axis=0, tiled=True)]
    reduce_scatter x1, waiting for transfers between devices: 36.1 us -> 0.01 us  [local(): lax.psum_scatter(key_part.astype(jnp.bfloat16), 'dp', scatter_dimension=0...]
    reduce_scatter x1, waiting for transfers between devices: 35 us -> 0.02 us  [local(): lax.psum_scatter(value_part.astype(jnp.bfloat16), 'dp', scatter_dimension...]
  transfers between devices with their start and end apart: 20 -> 22, of which waited for: 17 -> 19; matrix products, arithmetic and copies ran while one was open for 22% -> 12% of each run, Pallas kernels for 0% -> 0%
where the time goes in v1:
time: 1500 us; the launch traced here: 1490 us
  waiting for transfers between devices  1000 us (67%)
  matrix products  255 us (17%)
  other arithmetic  69.7 us (5%)
  blocking collectives  67.2 us (4%)
  local copies, waits for them, and re-layouts  63.3 us (4%)
  between operations  15.1 us (1%)
    all_gather x1, waiting for transfers between devices, local(): normed_mid = lax.all_gather(normed_mid_local, 'tensor', axis=0, tiled=True)  82.8 us
    reduce_scatter x1, waiting for transfers between devices, local(): lax.psum_scatter((jnp.einsum('rc,dc->rd', query_rows, query_all, preferre...  77.2 us
    reduce_scatter x1, waiting for transfers between devices, local(): lax.psum_scatter((jnp.einsum('rf,df->rd', d_gate, gate_all, preferred_ele...  76.9 us
    reduce_scatter x1, waiting for transfers between devices, local(): lax.psum_scatter(jnp.dot(context, out_all, preferred_element_type=jnp.flo...  76.3 us
    reduce_scatter x1, waiting for transfers between devices, local(): lax.psum_scatter(gate_part.astype(jnp.bfloat16), 'dp', scatter_dimension=...  72 us
    reduce_scatter x1, waiting for transfers between devices, local(): lax.psum_scatter(down_part.astype(jnp.bfloat16), 'dp', scatter_dimension=...  71.8 us
    all_gather x1, waiting for transfers between devices, local(): cot_all = lax.all_gather(cotangent, 'tensor', axis=0, tiled=True)  67.8 us
    all_gather x1, waiting for transfers between devices, local(): normed_in = lax.all_gather(normed_local, 'tensor', axis=0, tiled=True)  60.3 us
  transfers between devices with their start and end apart: 22, of which 19 were waited for; matrix products, arithmetic and copies ran while one was open for 12% of the time, Pallas kernels for 0%

profile of v1, /device:TPU:0, one launch (start us, length us, event | category | flops | bytes accessed | tf_op | source)
XLA Modules:
  0.0 1485.3 jit_solution(5428923198007650896)
XLA Ops:
  12.9 11.3 all_gather.32
  24.3 9.8 all_gather.33
  34.7 60.3 %all-gather.9.cloned.1.call-done = bf16[1024,2048]{1,0:T(8,128)(2,1)} async-done(((bf16[256,2048]{1,0:T(8,128)(2,1)}), bf16[1024,2048]{1,0:T(8,128)(2,1)}) %all-gather.9.cloned.1.call-update) | async-done | bytes 4194320 | tf_op jit(solution)/shard_map/all_gather | solution.py:79
  98.7 24.4 %all-gather.11.cloned.1.call-done = bf16[2048,512]{1,0:T(8,128)(2,1)} async-done(((bf16[256,512]{1,0:T(8,128)(2,1)}), bf16[2048,512]{1,0:T(8,128)(2,1)}) %all-gather.11.cloned.1.call-update) | async-done | bytes 2097168 | tf_op jit(solution)/shard_map/all_gather | solution.py:81
  123.1 5.2 fusion.87
  132.5 30.9 %while.32 = (s32[]{:T(128)}, bf16[2,512,512]{2,1,0:T(8,128)(2,1)S(1)}, f32[2,2,4,512,1]{3,2,1,4,0:T(4,128)}, s32[2]{0:T(128)S(1)}, s32[1024]{0:T(1024)S(1)}, /*i...) while((s32[]{:T(128)}, ...), condition=%wide.region_4.5_spmd.clone, body=%wide.region_1.4_spmd.clone.sunk | while | flops 1121710592 | bytes 56244616 | solution.py:133
  153.8 4.4 fusion.159
  163.5 6.3 convolution_convert_fusion.4
  170.5 76.3 %reduce-scatter.12.cloned.1.call-done = bf16[256,2048]{1,0:T(8,128)(2,1)} async-done(((bf16[1024,2048]{1,0:T(8,128)(2,1)}), bf16[256,2048]{1,0:T(8,128)(2,1)}) %reduce-scatter.12.cloned.1.call-update) | async-done | bytes 1048592 | tf_op jit(solution)/shard_map/reduce_scatter | solution.py:135
  253.3 50.0 %all-gather.19.cloned.1.call-done = bf16[2048,2048]{1,0:T(8,128)(2,1)} async-done(((bf16[256,2048]{1,0:T(8,128)(2,1)}), bf16[2048,2048]{1,0:T(8,128)(2,1)}) %all-gather.19.cloned.1.call-update) | async-done | bytes 8388624 | tf_op jit(solution)/shard_map/all_gather | solution.py:146
  303.3 82.8 %all-gather.15.cloned.1.call-done = bf16[1024,2048]{1,0:T(8,128)(2,1)} async-done(((bf16[256,2048]{1,0:T(8,128)(2,1)}), bf16[1024,2048]{1,0:T(8,128)(2,1)}) %all-gather.15.cloned.1.call-update) | async-done | bytes 4194320 | tf_op jit(solution)/shard_map/all_gather | solution.py:143
  386.1 14.9 %fusion.90 = f32[1024,2048]{1,0:T(8,128)} fusion(bf16[1024,2048]{1,0:T(8,128)(2,1)} %all-gather.15.cloned.1.call-done, bf16[2048,2048]{1,0:T(8,128)(2,1)} %all-gather.19.cloned.1.call-done), kind=kOutput, calls=%fused_computation.149 | convolution fusion | flops 8589934592 | bytes 20971520 | tf_op jit(solution)/shard_map/dot_general | solution.py:150
  401.0 39.8 %all-gather.17.cloned.1.call-done = bf16[2048,2048]{1,0:T(8,128)(2,1)} async-done(((bf16[256,2048]{1,0:T(8,128)(2,1)}), bf16[2048,2048]{1,0:T(8,128)(2,1)}) %all-gather.17.cloned.1.call-update) | async-done | bytes 8388624 | tf_op jit(solution)/shard_map/all_gather | solution.py:145
  440.7 14.5 fusion.89
  455.3 67.8 %all-gather.23.cloned.1.call-done = bf16[1024,2048]{1,0:T(8,128)(2,1)} async-done(((bf16[256,2048]{1,0:T(8,128)(2,1)}), bf16[1024,2048]{1,0:T(8,128)(2,1)}) %all-gather.23.cloned.1.call-update) | async-done | bytes 4194320 | tf_op jit(solution)/shard_map/all_gather | solution.py:159
  523.1 56.3 %all-gather.21.cloned.1.call-done = bf16[2048,2048]{1,0:T(8,128)(2,1)} async-done(((bf16[2048,256]{1,0:T(8,128)(2,1)}), bf16[2048,2048]{1,0:T(8,128)(2,1)}) %all-gather.21.cloned.1.call-update) | async-done | bytes 8388624 | tf_op jit(solution)/shard_map/all_gather | solution.py:147
  579.3 21.7 %multiply_convert_fusion = (bf16[1024,2048]{1,0:T(8,128)(2,1)}, bf16[1024,2048]{1,0:T(8,128)(2,1)}, bf16[1024,2048]{1,0:T(8,128)(2,1)}) fusion(f32[1024,2048]{1,0:T(8,128)} %fusion.89, f32[1024,2048]{1,0:T(8,128)} %fusion.90, bf16[1024,2048]{1,0:T(8,128)(2,1)} %all-gather.23.cloned.1.call-done, bf16[2048,2048]{1,0:T(8,128)(2,1)} %all-gather.21.cloned.1.call-done), kind=kOutput, calls=%fused_computation.69 | convolution fusion | flops 8623489024 | bytes 41943040 | tf_op jit(solution)/shard_map/rd,fd->rf/dot_general | solution.py:160
  601.1 12.9 fusion.91
  614.0 12.9 add_convert_fusion.1
  626.9 76.9 %reduce-scatter.16.cloned.1.call-done = bf16[256,2048]{1,0:T(8,128)(2,1)} async-done(((bf16[1024,2048]{1,0:T(8,128)(2,1)}), bf16[256,2048]{1,0:T(8,128)(2,1)}) %reduce-scatter.16.cloned.1.call-update) | async-done | bytes 1048592 | tf_op jit(solution)/shard_map/reduce_scatter | solution.py:168
  711.3 25.1 %collective-permute-done = bf16[256,2048]{1,0:T(8,128)(2,1)S(1)} collective-permute-done((bf16[256,2048]{1,0:T(8,128)(2,1)}, bf16[256,2048]{1,0:T(8,128)(2,1)S(1)}, u32[]{:S(2)}, u32[]{:S(2)}) %collective-permute-start) | collective-permute-done | bytes 1048608 | tf_op jit(solution)/shard_map/ppermute | solution.py:20
  740.3 24.0 %collective-permute-done.1 = bf16[256,2048]{1,0:T(8,128)(2,1)S(1)} collective-permute-done((bf16[256,2048]{1,0:T(8,128)(2,1)S(1)}, bf16[256,2048]{1,0:T(8,128)(2,1)S(1)}, u32[]{:S(2)}, u32[]{:S(2)}) %collective-permute-start.1) | collective-permute-done | bytes 1048608 | tf_op jit(solution)/shard_map/ppermute | solution.py:20
  765.8 17.3 %collective-permute-done.2 = bf16[256,2048]{1,0:T(8,128)(2,1)S(1)} collective-permute-done((bf16[256,2048]{1,0:T(8,128)(2,1)}, bf16[256,2048]{1,0:T(8,128)(2,1)S(1)}, u32[]{:S(2)}, u32[]{:S(2)}) %collective-permute-start.2) | collective-permute-done | bytes 1048608 | tf_op jit(solution)/shard_map/ppermute | solution.py:22
  788.7 133.4 %while.33 = (s32[]{:T(128)}, f32[1024,2,64]{0,2,1:T(8,128)}, f32[1024,2,64]{0,2,1:T(8,128)}, f32[2,512,2,4,64]{1,0,4,3,2:T(2,128)}, s32[2]{0:T(128)S(1)}, /*inde...) while((s32[]{:T(128)}, f32[1024,2,64]{0,2,1:T(8,128)}, ...), condition=%wide.region_12.13_spmd.clone, body=%wide.region_10.12_spmd.clone.sunk | while | flops 2749755904 | bytes 176093744 | solution.py:217
  797.2 5.3 fusion.174
  802.5 10.9 fusion.171
  813.4 8.2 fusion.172
  828.2 6.0 fusion.175
  835.4 19.6 %dynamic_update_slice.31 = f32[2,512,2,4,64]{1,0,4,3,2:T(2,128)} dynamic-update-slice(f32[2,512,2,4,64]{1,0,4,3,2:T(2,128)} %get-tuple-element.599, f32[1,512,2,4,64]{1,0,4,3,2:T(1,128)S(1)} %copy.49, s32[]{:T(128)S(6)} %copy.73, s32[]{:T(128)} %constant.185.clone.1..sunk.1, s32[]{:T(128)} %constant.185.clone.1..sunk.1, s32[]{:T(128)} %constant.185.clone.1..sunk.1, s32[]{:T(128)} %constant.185.clone.1..sunk.1) | dynamic-update-slice | bytes 2097156 | tf_op jit(solution)/shard_map/while/body/jit(dynamic_update_index_in_dim)/dynamic_update_slice | solution.py:217
  863.0 6.3 fusion.174
  869.4 10.9 fusion.171
  880.2 8.2 fusion.172
  895.3 6.0 fusion.175
  902.4 19.6 %dynamic_update_slice.31 = f32[2,512,2,4,64]{1,0,4,3,2:T(2,128)} dynamic-update-slice(f32[2,512,2,4,64]{1,0,4,3,2:T(2,128)} %get-tuple-element.599, f32[1,512,2,4,64]{1,0,4,3,2:T(1,128)S(1)} %copy.49, s32[]{:T(128)S(6)} %copy.73, s32[]{:T(128)} %constant.185.clone.1..sunk.1, s32[]{:T(128)} %constant.185.clone.1..sunk.1, s32[]{:T(128)} %constant.185.clone.1..sunk.1, s32[]{:T(128)} %constant.185.clone.1..sunk.1) | dynamic-update-slice | bytes 2097156 | tf_op jit(solution)/shard_map/while/body/jit(dynamic_update_index_in_dim)/dynamic_update_slice | solution.py:217
  933.2 14.1 convolution_convert_fusion.1
  947.4 14.1 convolution_convert_fusion.2
  961.5 14.3 convolution_convert_fusion
  977.1 5.9 fusion.64
  999.8 13.8 convolution_convert_fusion.3
  1016.8 58.0 %reduce-scatter.30.cloned.1.call-done = bf16[256,2048]{1,0:T(8,128)(2,1)} async-done(((bf16[2048,2048]{1,0:T(8,128)(2,1)}), bf16[256,2048]{1,0:T(8,128)(2,1)}) %reduce-scatter.30.cloned.1.call-update) | async-done | bytes 1048592 | tf_op jit(solution)/shard_map/reduce_scatter | solution.py:260
  1077.6 72.0 %reduce-scatter.28.cloned.1.call-done = bf16[256,2048]{1,0:T(8,128)(2,1)} async-done(((bf16[2048,2048]{1,0:T(8,128)(2,1)}), bf16[256,2048]{1,0:T(8,128)(2,1)}) %reduce-scatter.28.cloned.1.call-update) | async-done | bytes 1048592 | tf_op jit(solution)/shard_map/reduce_scatter | solution.py:257
  1152.5 71.8 %reduce-scatter.32.cloned.1.call-done = bf16[2048,256]{1,0:T(8,128)(2,1)} async-done(((bf16[2048,2048]{1,0:T(8,128)(2,1)}), bf16[2048,256]{1,0:T(8,128)(2,1)}) %reduce-scatter.32.cloned.1.call-update) | async-done | bytes 1048592 | tf_op jit(solution)/shard_map/reduce_scatter | solution.py:263
  1227.0 41.6 %reduce-scatter.26.cloned.1.call-done = bf16[512,256]{1,0:T(8,128)(2,1)} async-done(((bf16[512,2048]{1,0:T(8,128)(2,1)}), bf16[512,256]{1,0:T(8,128)(2,1)}) %reduce-scatter.26.cloned.1.call-update) | async-done | bytes 262160 | tf_op jit(solution)/shard_map/reduce_scatter | solution.py:254
  1270.4 43.1 %reduce-scatter.20.cloned.1.call-done = bf16[256,512]{1,0:T(8,128)(2,1)} async-done(((bf16[2048,512]{1,0:T(8,128)(2,1)}), bf16[256,512]{1,0:T(8,128)(2,1)}) %reduce-scatter.20.cloned.1.call-update) | async-done | bytes 262160 | tf_op jit(solution)/shard_map/reduce_scatter | solution.py:245
  1315.2 77.2 %reduce-scatter.18.cloned.1.call-done = bf16[256,2048]{1,0:T(8,128)(2,1)} async-done(((bf16[1024,2048]{1,0:T(8,128)(2,1)}), bf16[256,2048]{1,0:T(8,128)(2,1)}) %reduce-scatter.18.cloned.1.call-update) | async-done | bytes 1048592 | tf_op jit(solution)/shard_map/reduce_scatter | solution.py:230
  1394.7 46.0 %all-reduce.4 = (f32[2048]{0:T(1024)}, f32[2048]{0:T(1024)}) all-reduce(f32[2048]{0:T(1024)S(1)} %get-tuple-element.341, f32[2048]{0:T(1024)S(1)} %copy-done.28), channel_id=1, replica_groups=mesh['dp'=8,'tensor'=4] {'dp','tensor'}, use_global_device_ids=true, to_apply=%region_16.17 | all-reduce | flops 4096 | bytes 32768 | tf_op jit(solution)/shard_map/psum | solution.py:243
  1440.7 32.4 %reduce-scatter.14.cloned.1.call-done = bf16[256,2048]{1,0:T(8,128)(2,1)} async-done(((bf16[1024,2048]{1,0:T(8,128)(2,1)}), bf16[256,2048]{1,0:T(8,128)(2,1)}) %reduce-scatter.14.cloned.1.call-update) | async-done | bytes 1048592 | tf_op jit(solution)/shard_map/reduce_scatter | solution.py:152
  1473.1 5.1 fusion.76
  (226 shorter events, 137.2 us)
Async XLA Ops:
  7.2 17.1 %copy-start.27 = (bf16[256,128]{1,0:T(8,128)(2,1)S(1)}, bf16[256,128]{1,0:T(8,128)(2,1)}, u32[]{:S(2)}) copy-start(bf16[256,128]{1,0:T(8,128)(2,1)} %param.23) | copy-start | bytes 196612
  7.2 87.7 %all-gather.9.cloned.1.call-start = ((), (), s32[]{:S(2)}) async-start(), calls=%async_computation.11 | async-start | bytes 5242880 | tf_op jit(solution)/shard_map/all_gather | solution.py:79
  8.8 15.5 %copy-start.35 = (f32[256]{0:T(256)}, f32[256]{0:T(256)S(1)}, u32[]{:S(2)}) copy-start(f32[256]{0:T(256)S(1)} %fusion.77) | copy-start | bytes 3076
  8.8 15.5 %copy-start.31 = (f32[256]{0:T(256)}, f32[256]{0:T(256)S(1)}, u32[]{:S(2)}) copy-start(f32[256]{0:T(256)S(1)} %fusion.82) | copy-start | bytes 3076
  11.3 111.8 %all-gather.11.cloned.1.call-start = ((), (), s32[]{:S(2)}) async-start(), calls=%async_computation.12 | async-start | bytes 2359296 | tf_op jit(solution)/shard_map/all_gather | solution.py:81
  12.1 151.4 %all-gather.13.cloned.1.call-start = ((), (), s32[]{:S(2)}) async-start(), calls=%async_computation.13 | async-start | bytes 2359296 | tf_op jit(solution)/shard_map/all_gather | solution.py:84
  12.8 233.9 %reduce-scatter.12.cloned.1.call-start = ((), (), s32[]{:S(2)}) async-start(), calls=%async_computation.14 | async-start | bytes 5242880 | tf_op jit(solution)/shard_map/reduce_scatter | solution.py:135
  24.3 104.1 %copy-start.14 = (bf16[2048,128]{1,0:T(8,128)(2,1)}, bf16[2048,128]{1,0:T(8,128)(2,1)S(1)}, u32[]{:S(2)}) copy-start(bf16[2048,128]{1,0:T(8,128)(2,1)S(1)} %all_gather.32) | copy-start | bytes 1572868
  34.1 95.8 %copy-start.12 = (bf16[2048,128]{1,0:T(8,128)(2,1)}, bf16[2048,128]{1,0:T(8,128)(2,1)S(1)}, u32[]{:S(2)}) copy-start(bf16[2048,128]{1,0:T(8,128)(2,1)S(1)} %all_gather.33) | copy-start | bytes 1572868
  34.6 93.8 %copy-start.17 = (f32[1024,32]{0,1:T(8,128)}, f32[1024,32]{0,1:T(8,128)S(1)}, u32[]{:S(2)}) copy-start(f32[1024,32]{0,1:T(8,128)S(1)} %get-tuple-element.402) | copy-start | bytes 393220
  34.6 93.8 %copy-start.19 = (f32[1024,32]{0,1:T(8,128)}, f32[1024,32]{0,1:T(8,128)S(1)}, u32[]{:S(2)}) copy-start(f32[1024,32]{0,1:T(8,128)S(1)} %get-tuple-element.403) | copy-start | bytes 393220
  163.4 6.4 copy-start.7
  163.4 6.4 copy-start.40
  169.8 77.0 %copy-start.1 = (bf16[256,2048]{1,0:T(8,128)(2,1)S(1)}, bf16[256,2048]{1,0:T(8,128)(2,1)}, u32[]{:S(2)}) copy-start(bf16[256,2048]{1,0:T(8,128)(2,1)} %param.17) | copy-start | bytes 3145732
  169.8 78.6 %copy-start.23 = (f32[2048]{0:T(1024)S(1)}, f32[2048]{0:T(1024)}, u32[]{:S(2)}) copy-start(f32[2048]{0:T(1024)} %param.25) | copy-start | bytes 24580
  169.8 133.5 %all-gather.19.cloned.1.call-start = ((), (), s32[]{:S(2)}) async-start(), calls=%async_computation.17 | async-start | bytes 9437184 | tf_op jit(solution)/shard_map/all_gather | solution.py:146
  170.4 215.7 %all-gather.15.cloned.1.call-start = ((), (), s32[]{:S(2)}) async-start(), calls=%async_computation.15 | async-start | bytes 5242880 | tf_op jit(solution)/shard_map/all_gather | solution.py:143
  248.4 458.2 %copy-start.29 = (f32[256]{0:T(256)}, f32[256]{0:T(256)S(1)}, u32[]{:S(2)}) copy-start(f32[256]{0:T(256)S(1)} %fusion.83) | copy-start | bytes 3076
  251.0 189.7 %all-gather.17.cloned.1.call-start = ((), (), s32[]{:S(2)}) async-start(), calls=%async_computation.16 | async-start | bytes 9437184 | tf_op jit(solution)/shard_map/all_gather | solution.py:145
  251.8 271.3 %all-gather.23.cloned.1.call-start = ((), (), s32[]{:S(2)}) async-start(), calls=%async_computation.20 | async-start | bytes 5242880 | tf_op jit(solution)/shard_map/all_gather | solution.py:159
  252.5 326.8 %all-gather.21.cloned.1.call-start = ((), (), s32[]{:S(2)}) async-start(), calls=%async_computation.18 | async-start | bytes 9437184 | tf_op jit(solution)/shard_map/all_gather | solution.py:147
  253.3 450.6 %reduce-scatter.16.cloned.1.call-start = ((), (), s32[]{:S(2)}) async-start(), calls=%async_computation.21 | async-start | bytes 5242880 | tf_op jit(solution)/shard_map/reduce_scatter | solution.py:168
  601.1 12.9 copy-start.42
  626.9 77.0 %copy-start.3 = (bf16[256,2048]{1,0:T(8,128)(2,1)S(1)}, bf16[256,2048]{1,0:T(8,128)(2,1)}, u32[]{:S(2)}) copy-start(bf16[256,2048]{1,0:T(8,128)(2,1)} %reduce-scatter.12.cloned.1.call-done) | copy-start | bytes 3145732
  626.9 79.8 %copy-start.9 = (bf16[256,2048]{1,0:T(8,128)(2,1)S(1)}, bf16[256,2048]{1,0:T(8,128)(2,1)}, u32[]{:S(2)}) copy-start(bf16[256,2048]{1,0:T(8,128)(2,1)} %param.29) | copy-start | bytes 3145732
  626.9 386.8 %reduce-scatter.24.cloned.1.call-start = ((), (), s32[]{:S(2)}) async-start(), calls=%async_computation.25 | async-start | bytes 589824 | tf_op jit(solution)/shard_map/reduce_scatter | solution.py:251
  706.6 57.8 %copy-start.33 = (f32[256]{0:T(256)}, f32[256]{0:T(256)S(1)}, u32[]{:S(2)}) copy-start(f32[256]{0:T(256)S(1)} %multiply_multiply_fusion.1) | copy-start | bytes 3076
  709.8 26.6 %collective-permute-start = (bf16[256,2048]{1,0:T(8,128)(2,1)}, bf16[256,2048]{1,0:T(8,128)(2,1)S(1)}, u32[]{:S(2)}, u32[]{:S(2)}) collective-permute-start(bf16[256,2048]{1,0:T(8,128)(2,1)} %fusion.86), channel_id=1, source_target_pairs={{0,1},{1,2},{2,3},{3,0},{4,5},{5,6},{6,7},{7,4},{8,9},{9,10},{10,1... | collective-permute-start | bytes 3145736 | tf_op jit(solution)/shard_map/ppermute | solution.py:20
  736.4 27.8 %collective-permute-start.1 = (bf16[256,2048]{1,0:T(8,128)(2,1)S(1)}, bf16[256,2048]{1,0:T(8,128)(2,1)S(1)}, u32[]{:S(2)}, u32[]{:S(2)}) collective-permute-start(bf16[256,2048]{1,0:T(8,128)(2,1)S(1)} %collective-permute-done), channel_id=1, source_target_pairs={{0,1},{1,2},{2,3},{3,0},{4,5},{5,6},{6,7},{7,4},{8,9},{9,10},{10,1... | collective-permute-start | bytes 3145736 | tf_op jit(solution)/shard_map/ppermute | solution.py:20
  736.4 46.6 %collective-permute-start.2 = (bf16[256,2048]{1,0:T(8,128)(2,1)}, bf16[256,2048]{1,0:T(8,128)(2,1)S(1)}, u32[]{:S(2)}, u32[]{:S(2)}) collective-permute-start(bf16[256,2048]{1,0:T(8,128)(2,1)} %fusion.86), channel_id=1, source_target_pairs={{0,3},{1,0},{2,1},{3,2},{4,7},{5,4},{6,5},{7,6},{8,11},{9,8},{10,9... | collective-permute-start | bytes 3145736 | tf_op jit(solution)/shard_map/ppermute | solution.py:22
  927.6 87.7 %reduce-scatter.22.cloned.1.call-start = ((), (), s32[]{:S(2)}) async-start(), calls=%async_computation.24 | async-start | bytes 589824 | tf_op jit(solution)/shard_map/reduce_scatter | solution.py:248
  933.2 141.7 %reduce-scatter.30.cloned.1.call-start = ((), (), s32[]{:S(2)}) async-start(), calls=%async_computation.28 | async-start | bytes 9437184 | tf_op jit(solution)/shard_map/reduce_scatter | solution.py:260
  947.3 202.4 %reduce-scatter.28.cloned.1.call-start = ((), (), s32[]{:S(2)}) async-start(), calls=%async_computation.27 | async-start | bytes 9437184 | tf_op jit(solution)/shard_map/reduce_scatter | solution.py:257
  961.5 262.9 %reduce-scatter.32.cloned.1.call-start = ((), (), s32[]{:S(2)}) async-start(), calls=%async_computation.29 | async-start | bytes 9437184 | tf_op jit(solution)/shard_map/reduce_scatter | solution.py:263
  975.8 292.7 %reduce-scatter.26.cloned.1.call-start = ((), (), s32[]{:S(2)}) async-start(), calls=%async_computation.26 | async-start | bytes 2359296 | tf_op jit(solution)/shard_map/reduce_scatter | solution.py:254
  983.0 330.4 %reduce-scatter.20.cloned.1.call-start = ((), (), s32[]{:S(2)}) async-start(), calls=%async_computation.23 | async-start | bytes 2359296 | tf_op jit(solution)/shard_map/reduce_scatter | solution.py:245
  992.2 400.2 %reduce-scatter.18.cloned.1.call-start = ((), (), s32[]{:S(2)}) async-start(), calls=%async_computation.22 | async-start | bytes 5242880 | tf_op jit(solution)/shard_map/reduce_scatter | solution.py:230
  999.8 473.3 %reduce-scatter.14.cloned.1.call-start = ((), (), s32[]{:S(2)}) async-start(), calls=%async_computation.19 | async-start | bytes 5242880 | tf_op jit(solution)/shard_map/reduce_scatter | solution.py:152
  1077.6 314.8 %copy-start.2 = (bf16[256,2048]{1,0:T(8,128)(2,1)S(1)}, bf16[256,2048]{1,0:T(8,128)(2,1)}, u32[]{:S(2)}) copy-start(bf16[256,2048]{1,0:T(8,128)(2,1)} %param.17) | copy-start | bytes 3145732
  1077.6 314.8 %copy-start.25 = (f32[2048]{0:T(1024)S(1)}, f32[2048]{0:T(1024)}, u32[]{:S(2)}) copy-start(f32[2048]{0:T(1024)} %param.20) | copy-start | bytes 24580
  1077.6 314.8 %copy-start.32 = (f32[256]{0:T(256)S(1)}, f32[256]{0:T(256)}, u32[]{:S(2)}) copy-start(f32[256]{0:T(256)} %copy-done.31) | copy-start | bytes 3076
  1152.5 242.2 %copy-start.28 = (f32[2048]{0:T(1024)S(1)}, f32[2048]{0:T(1024)}, u32[]{:S(2)}) copy-start(f32[2048]{0:T(1024)} %get-tuple-element.339) | copy-start | bytes 24580
  1152.5 288.2 %copy-start.36 = (f32[256]{0:T(256)S(1)}, f32[256]{0:T(256)}, u32[]{:S(2)}) copy-start(f32[256]{0:T(256)} %copy-done.35) | copy-start | bytes 3076
  1152.5 320.6 %copy-start.4 = (bf16[256,2048]{1,0:T(8,128)(2,1)S(1)}, bf16[256,2048]{1,0:T(8,128)(2,1)}, u32[]{:S(2)}) copy-start(bf16[256,2048]{1,0:T(8,128)(2,1)} %reduce-scatter.12.cloned.1.call-done) | copy-start | bytes 3145732
  1152.5 320.7 %copy-start.10 = (bf16[256,2048]{1,0:T(8,128)(2,1)S(1)}, bf16[256,2048]{1,0:T(8,128)(2,1)}, u32[]{:S(2)}) copy-start(bf16[256,2048]{1,0:T(8,128)(2,1)} %param.29) | copy-start | bytes 3145732
  1152.5 320.6 %copy-start.24 = (f32[2048]{0:T(1024)S(1)}, f32[2048]{0:T(1024)}, u32[]{:S(2)}) copy-start(f32[2048]{0:T(1024)} %param.25) | copy-start | bytes 24580
  1152.5 320.6 %copy-start.30 = (f32[256]{0:T(256)S(1)}, f32[256]{0:T(256)}, u32[]{:S(2)}) copy-start(f32[256]{0:T(256)} %copy-done.29) | copy-start | bytes 3076
  1152.5 320.6 %copy-start.34 = (f32[256]{0:T(256)S(1)}, f32[256]{0:T(256)}, u32[]{:S(2)}) copy-start(f32[256]{0:T(256)} %copy-done.33) | copy-start | bytes 3076
  (20 other events, 71.3 us)
Sparse Core Ops, SparseCore 0:
  11.4 83.4 all-gather.8
  96.8 26.2 all-gather.10
  125.0 28.1 all-gather.12
  170.0 76.7 reduce-scatter.11
  248.5 54.7 all-gather.18
  305.3 80.7 all-gather.14
  388.0 52.7 all-gather.16
  442.3 80.7 all-gather.22
  525.0 54.3 all-gather.20
  627.0 76.7 reduce-scatter.15
  927.7 34.3 reduce-scatter.23
  965.7 34.1 reduce-scatter.21
  1003.3 71.4 reduce-scatter.29
  1078.1 71.4 reduce-scatter.27
  1153.0 71.2 reduce-scatter.31
  1227.4 41.0 reduce-scatter.25
  1272.3 41.1 reduce-scatter.19
  1315.6 76.7 reduce-scatter.17
  1394.7 78.3 reduce-scatter.13
